TPU v7x, 128 devices: a whole 4x4x4 slice. The times are simulated.
128 devices in a mesh: req: 32 (over x, z, core), mlp: 4 (over y).
Axes of the slice: x: 4, y: 4, z: 4, core: 2. Of those that a mesh axis runs over, the one named last changes fastest.
Arguments:
- queries: bfloat16 [16896, 2048], P('req', 'mlp'), may hold values from -6 to 6
- key_cache: bfloat16 [2560, 128, 1024], P('req', None, 'mlp'), may hold values from -6 to 6
- value_cache: bfloat16 [2560, 128, 1024], P('req', None, 'mlp'), may hold values from -6 to 6
- decode_len: int32 [512], P('req'), may hold values from 1 to 4096, as said below
- stretch_start: int32 [32], P('req'), may hold values from 0 to 3584, as said below
- page_table: int32 [544, 32], P('req'), may hold values from 0 to 79, as said below
- hidden_in: bfloat16 [16896, 2304], P('req')
- o_weight: bfloat16 [2048, 2304], P('mlp'), may hold values from -0.125 to 0.125
- attn_gain: float32 [2304], replicated, may hold values from 0.1 to 1.9
- ffn_in_gain: float32 [2304], replicated, may hold values from 0.1 to 1.9
- ffn_out_gain: float32 [2304], replicated, may hold values from 0.1 to 1.9
- w_gate: bfloat16 [2304, 9216], P('req', 'mlp'), may hold values from -0.125 to 0.125
- w_up: bfloat16 [2304, 9216], P('req', 'mlp'), may hold values from -0.125 to 0.125
- w_down: bfloat16 [2304, 9216], P('req', 'mlp')
Outputs:
- layer_out: bfloat16 [16896, 2304], P('req', 'mlp')
Inputs may be any that keep to these rules, and one draw needn't show every extreme that they name: `decode_len`: each decode request's tokens fill its first pages; request 1 of req index 1 holds 4096 tokens. `stretch_start`: req index 0 starts at 3584, req index 1 at 0. `page_table`: row j of req index r's block of 17 rows names request j's pages by slot in that index's own pool of 80 pages; the slots holding a req index's tokens are all distinct; entries past a request's last page are valid slots that hold none of its tokens.
All inputs are finite; a program needn't handle non-finite values.
Results may differ from a plain program's by a relative error of at most 0.014.
Values may be sent and summed in bfloat16 or wider, within the bound.
A program may use at most 128 MiB of HBM per device.

v0:
```python
import math
import jax
import jax.numpy as jnp
from jax import lax
from jax.sharding import PartitionSpec as P

H = 8
KVH = 4
HD = 256
PRE_DEV = 512
DEC_DEV = 16
EPS = 1e-06
CAP = 50.0


def rms(values, gain):
    return values * lax.rsqrt(jnp.mean(values * values, axis=-1, keepdims=True) + EPS) * gain


def capped_weight(scores, visible):
    capped = CAP * jnp.tanh(scores / (16.0 * CAP))
    return jnp.where(visible, jnp.exp(capped), jnp.float32(0.0))


def attend(queries, key_cache, value_cache, decode_len, stretch_start, page_table):
    rows = queries.shape[0]
    local_kv = key_cache.shape[2] // HD
    rep = H // KVH
    pool = key_cache.shape[0]
    page_len = key_cache.shape[1]
    max_pages = page_table.shape[1]
    query = queries.reshape(rows, local_kv, rep, HD)
    pre_q = query[:PRE_DEV]
    dec_q = query[PRE_DEV:]
    start = stretch_start[0]
    pre_keys = key_cache[page_table[0]].reshape(max_pages * page_len, local_kv, HD)
    pre_vals = value_cache[page_table[0]].reshape(max_pages * page_len, local_kv, HD)
    position = jnp.arange(max_pages * page_len, dtype=jnp.int32)
    limit = start + jnp.arange(PRE_DEV, dtype=jnp.int32) + 1
    pre_scores = jnp.einsum("rghd,tgd->rght", pre_q, pre_keys, preferred_element_type=jnp.float32)
    pre_weight = capped_weight(
        pre_scores, position[None, None, None, :] < limit[:, None, None, None]
    )
    pre_num = jnp.einsum(
        "rght,tgd->rghd",
        pre_weight.astype(jnp.bfloat16),
        pre_vals,
        preferred_element_type=jnp.float32,
    )
    pre_den = jnp.sum(pre_weight, axis=-1)
    table = page_table[1:]
    page_idx = jnp.arange(max_pages, dtype=jnp.int32)
    used = page_idx[None, :] * page_len < decode_len[:, None]
    owned = (table[:, :, None] == jnp.arange(pool, dtype=jnp.int32)[None, None, :]) & used[
        :, :, None
    ]
    base = jnp.min(jnp.where(owned, page_idx[None, :, None] * page_len, jnp.int32(1 << 30)), axis=1)
    dec_pos = (base[:, :, None] + jnp.arange(page_len, dtype=jnp.int32)[None, None, :]).reshape(
        DEC_DEV, pool * page_len
    )
    all_keys = key_cache.reshape(pool * page_len, local_kv, HD)
    all_vals = value_cache.reshape(pool * page_len, local_kv, HD)
    dec_scores = jnp.einsum("rghd,tgd->rght", dec_q, all_keys, preferred_element_type=jnp.float32)
    dec_weight = capped_weight(dec_scores, (dec_pos < decode_len[:, None])[:, None, None, :])
    dec_num = jnp.einsum(
        "rght,tgd->rghd",
        dec_weight.astype(jnp.bfloat16),
        all_vals,
        preferred_element_type=jnp.float32,
    )
    dec_den = jnp.sum(dec_weight, axis=-1)
    pre_out = (pre_num / pre_den[..., None]).astype(jnp.bfloat16)
    dec_out = (dec_num / dec_den[..., None]).astype(jnp.bfloat16)
    return jnp.concatenate([pre_out, dec_out], axis=0).reshape(rows, local_kv * rep * HD)


def per_device(
    queries,
    key_cache,
    value_cache,
    decode_len,
    stretch_start,
    page_table,
    hidden_in,
    o_weight,
    attn_gain,
    ffn_in_gain,
    ffn_out_gain,
    w_gate,
    w_up,
    w_down,
):
    attended = attend(queries, key_cache, value_cache, decode_len, stretch_start, page_table)
    projected = lax.psum(
        jnp.dot(attended, o_weight, preferred_element_type=jnp.float32).astype(jnp.bfloat16), "mlp"
    ).astype(jnp.float32)
    resid = hidden_in.astype(jnp.float32) + rms(projected, attn_gain)
    normed = rms(resid, ffn_in_gain).astype(jnp.bfloat16)
    gate = jnp.dot(
        normed,
        lax.all_gather(w_gate, "req", axis=0, tiled=True),
        preferred_element_type=jnp.float32,
    )
    up_part = jnp.dot(
        normed, lax.all_gather(w_up, "req", axis=0, tiled=True), preferred_element_type=jnp.float32
    )
    act = (jax.nn.gelu(gate, approximate=True) * up_part).astype(jnp.bfloat16)
    partial_out = lax.dot_general(
        act,
        lax.all_gather(w_down, "req", axis=0, tiled=True),
        (((1,), (1,)), ((), ())),
        preferred_element_type=jnp.float32,
    )
    width = hidden_in.shape[1] // lax.axis_size("mlp")
    first = lax.axis_index("mlp") * width
    total = lax.psum(partial_out.astype(jnp.bfloat16), "mlp").astype(jnp.float32)
    combined = resid + rms(total, ffn_out_gain)
    result = lax.dynamic_slice_in_dim(combined, first, width, 1)
    return result.astype(jnp.bfloat16)


def solution(mesh):
    return jax.shard_map(
        per_device,
        mesh=mesh,
        in_specs=(
            P("req", "mlp"),
            P("req", None, "mlp"),
            P("req", None, "mlp"),
            P("req"),
            P("req"),
            P("req", None),
            P("req", None),
            P("mlp", None),
            P(),
            P(),
            P(),
            P("req", "mlp"),
            P("req", "mlp"),
            P("req", "mlp"),
        ),
        out_specs=P("req", "mlp"),
        check_vma=False,
    )
```

profile of v0, /device:TPU:1, one launch (start us, length us, event | category | flops | bytes accessed | tf_op | source)
XLA Modules:
  0.0 324.8 jit_solution(14163465529039394121)
XLA Ops:
  7.4 0.8 fusion.41
  8.2 0.7 slice.17
  8.9 1.1 slice.16
  10.7 3.0 iota_compare_fusion
  13.7 0.2 copy.35
  13.9 4.5 %gather_fusion.1 = bf16[32,128,256]{2,1,0:T(8,128)(2,1)} fusion(bf16[80,128,256]{2,1,0:T(8,128)(2,1)} %param.15, s32[1024]{0:T(1024)S(1)} %pad_clamp_fusion), kind=kCustom, calls=%fused_computation.1 | custom fusion | bytes 4194432 | tf_op jit(solution)/shard_map/gather | solution.py:36
  18.4 4.5 %gather_fusion = bf16[32,128,256]{2,1,0:T(8,128)(2,1)} fusion(bf16[80,128,256]{2,1,0:T(8,128)(2,1)} %param.16, s32[1024]{0:T(1024)S(1)} %pad_clamp_fusion), kind=kCustom, calls=%fused_computation | custom fusion | bytes 4194432 | tf_op jit(solution)/shard_map/gather | solution.py:37
  22.9 0.1 broadcast_compare_fusion
  23.0 0.2 select_reduce_fusion
  23.2 0.2 add.106
  23.5 0.3 fusion.35
  23.8 10.4 %fusion = (f32[512,2]{0,1:T(2,128)S(1)}, f32[4096,512,2]{1,0,2:T(8,128)}) fusion(pred[512,4096]{0,1:T(8,128)(4,1)} %iota_compare_fusion, bf16[4096,256,1]{1,0,2:T(8,128)(2,1)} %bitcast.101, bf16[512,2,256]{0,2,1:T(8,128)(2,1)S(1)} %bitcast.110), kind=kOutput, calls=%fused_computation.3 | convolution fusion | flops 2164259840 | bytes 21499904 | tf_op jit(solution)/shard_map/rghd,tgd->rght/dot_general | solution.py:40
  34.3 9.5 %fusion.32 = bf16[512,1,2,256]{0,3,2,1:T(8,128)(2,1)S(1)} fusion(bf16[4096,256,1]{1,0,2:T(8,128)(2,1)S(1)} %bitcast.100, f32[4096,512,2]{1,0,2:T(8,128)} %get-tuple-element.10, pred[512,4096]{0,1:T(8,128)(4,1)S(1)} %copy-done.2, f32[512,2]{0,1:T(2,128)S(1)} %get-tuple-element.9), kind=kOutput, calls=%fused_computation.45 | convolution fusion | flops 2164785152 | bytes 21499904 | tf_op jit(solution)/shard_map/rght,tgd->rghd/dot_general | solution.py:44
  43.9 1.8 fusion.47
  45.6 2.1 fusion.29
  47.9 2.9 convolution_convert_fusion.1
  50.8 0.5 all-gather.4.cloned.1.call-update
  51.4 0.5 all-gather.6.cloned.1.call-update
  52.0 0.5 all-gather.8.cloned.1.call-update
  52.6 65.7 %all-reduce.3.cloned.1.call-done = bf16[528,2304]{1,0:T(8,128)(2,1)} async-done(((bf16[528,2304]{1,0:T(8,128)(2,1)}), bf16[528,2304]{1,0:T(8,128)(2,1)}) %all-reduce.3.cloned.1.call-update) | async-done | bytes 2433040 | tf_op jit(solution)/shard_map/psum | solution.py:94
  118.2 2.2 fusion.11
  120.5 5.8 %multiply_reduce_fusion.1 = (f32[528]{0:T(1024)S(1)}, f32[528,2304]{1,0:T(8,128)}) fusion(f32[2304]{0:T(1024)S(1)} %copy-done.4, f32[528]{0:T(1024)S(1)} %add_rsqrt_fusion.2, bf16[528,2304]{1,0:T(8,128)(2,1)} %all-reduce.3.cloned.1.call-done, bf16[528,2304]{1,0:T(8,128)(2,1)} %param.20), kind=kLoop, calls=%fused_computation.31 | loop fusion | flops 8515056 | bytes 9745536 | tf_op jit(solution)/shard_map/reduce_sum | solution.py:17
  126.3 12.7 %fusion.45 = f32[528,2304]{1,0:T(8,128)} fusion(bf16[2304,2304]{1,0:T(8,128)(2,1)} %all-gather.4.cloned.1.call-done, f32[528,2304]{1,0:T(8,128)} %get-tuple-element.6, f32[2304]{0:T(1024)S(1)} %copy-done.6, f32[528]{0:T(1024)S(1)} %add_rsqrt_fusion.1), kind=kOutput, calls=%fused_computation.69 | convolution fusion | flops 5609336832 | bytes 20360256 | tf_op jit(solution)/shard_map/dot_general | solution.py:99
  139.0 36.0 %all-gather.6.cloned.1.call-done = bf16[2304,2304]{1,0:T(8,128)(2,1)} async-done(((bf16[72,2304]{1,0:T(8,128)(2,1)}), bf16[2304,2304]{1,0:T(8,128)(2,1)}) %all-gather.6.cloned.1.call-update) | async-done | bytes 10616848 | tf_op jit(solution)/shard_map/all_gather | solution.py:105
  175.0 12.9 %fusion.21 = bf16[528,2304]{1,0:T(8,128)(2,1)} fusion(bf16[2304,2304]{1,0:T(8,128)(2,1)} %all-gather.6.cloned.1.call-done, f32[528,2304]{1,0:T(8,128)} %fusion.45, f32[528,2304]{1,0:T(8,128)} %get-tuple-element.6, f32[2304]{0:T(1024)S(1)} %copy-done.6, f32[528]{0:T(1024)S(1)} %add_rsqrt_fusion.1), kind=kOutput, calls=%fused_computation.32 | convolution fusion | flops 5621501952 | bytes 22793280 | tf_op jit(solution)/shard_map/dot_general | solution.py:104
  187.8 46.8 %all-gather.8.cloned.1.call-done = bf16[2304,2304]{1,0:T(8,128)(2,1)} async-done(((bf16[72,2304]{1,0:T(8,128)(2,1)}), bf16[2304,2304]{1,0:T(8,128)(2,1)}) %all-gather.8.cloned.1.call-update) | async-done | bytes 10616848 | tf_op jit(solution)/shard_map/all_gather | solution.py:110
  234.7 11.6 %convolution_convert_fusion = bf16[528,2304]{1,0:T(8,128)(2,1)} fusion(bf16[528,2304]{1,0:T(8,128)(2,1)} %fusion.21, bf16[2304,2304]{1,0:T(8,128)(2,1)} %all-gather.8.cloned.1.call-done), kind=kOutput, calls=%fused_computation.33 | convolution fusion | flops 5606903808 | bytes 15482880 | tf_op jit(solution)/shard_map/dot_general | solution.py:108
  246.3 0.8 dynamic-slice
  247.1 62.5 %all-reduce.5.cloned.1.call-done = bf16[528,2304]{1,0:T(8,128)(2,1)} async-done(((bf16[528,2304]{1,0:T(8,128)(2,1)}), bf16[528,2304]{1,0:T(8,128)(2,1)}) %all-reduce.5.cloned.1.call-update) | async-done | bytes 2433040 | tf_op jit(solution)/shard_map/psum | solution.py:116
  309.6 2.2 multiply_reduce_fusion
  311.9 2.2 convert_element_type.54
  314.1 3.2 fusion.25
  (42 shorter events, 0.4 us)
Async XLA Ops:
  7.4 40.5 %copy-start = (bf16[512,2304]{1,0:T(8,128)(2,1)S(1)}, bf16[512,2304]{1,0:T(8,128)(2,1)}, u32[]{:S(2)}) copy-start(bf16[512,2304]{1,0:T(8,128)(2,1)} %param.21) | copy-start | bytes 7077892
  7.4 110.9 %all-reduce.3.cloned.1.call-start = ((), (), s32[]{:S(2)}) async-start(), calls=%async_computation | async-start | bytes 4866048 | tf_op jit(solution)/shard_map/psum | solution.py:94
  13.7 9.2 %copy-start.5 = (s32[16]{0:T(128)S(1)}, s32[16]{0:T(128)}, u32[]{:S(2)}) copy-start(s32[16]{0:T(128)} %param.17) | copy-start | bytes 196
  23.7 10.5 %copy-start.2 = (pred[512,4096]{0,1:T(8,128)(4,1)S(1)}, pred[512,4096]{0,1:T(8,128)(4,1)}, u32[]{:S(2)}) copy-start(pred[512,4096]{0,1:T(8,128)(4,1)} %iota_compare_fusion) | copy-start | bytes 6291460
  23.7 10.5 %copy-start.3 = (bf16[32,128,256]{2,1,0:T(8,128)(2,1)S(1)}, bf16[32,128,256]{2,1,0:T(8,128)(2,1)}, u32[]{:S(2)}) copy-start(bf16[32,128,256]{2,1,0:T(8,128)(2,1)} %gather_fusion) | copy-start | bytes 6291460
  23.8 20.1 %slice-start = ((s8[5242880]{0:T(1024)(128)(4,1)}), s8[4194304]{0:T(1024)(128)(4,1)S(1)}, s32[]{:S(2)}) async-start(s8[5242880]{0:T(1024)(128)(4,1)} %bitcast.102), calls=%async_computation.5 | async-start | bytes 8388608
  23.8 21.8 %slice-start.2 = ((s8[5242880]{0:T(1024)(128)(4,1)}), s8[4194304]{0:T(1024)(128)(4,1)S(1)}, s32[]{:S(2)}) async-start(s8[5242880]{0:T(1024)(128)(4,1)} %bitcast.105), calls=%async_computation.7 | async-start | bytes 8388608
  34.2 9.6 %slice-start.1 = ((s8[5242880]{0:T(1024)(128)(4,1)}), s8[1048576]{0:T(1024)(128)(4,1)S(1)}, s32[]{:S(2)}) async-start(s8[5242880]{0:T(1024)(128)(4,1)} %bitcast.102), calls=%async_computation.6 | async-start | bytes 2097152
  34.2 9.6 %slice-start.4 = ((bf16[528,512]{1,0:T(8,128)(2,1)}), bf16[16,512]{1,0:T(8,128)(2,1)S(1)}, s32[]{:S(2)}) async-start(bf16[528,512]{1,0:T(8,128)(2,1)} %param.14), calls=%async_computation.9 | async-start | bytes 32768 | tf_op jit(solution)/shard_map/slice | solution.py:34
  34.3 11.4 %slice-start.3 = ((s8[5242880]{0:T(1024)(128)(4,1)}), s8[1048576]{0:T(1024)(128)(4,1)S(1)}, s32[]{:S(2)}) async-start(s8[5242880]{0:T(1024)(128)(4,1)} %bitcast.105), calls=%async_computation.8 | async-start | bytes 2097152
  50.7 69.7 %copy-start.4 = (f32[2304]{0:T(1024)S(1)}, f32[2304]{0:T(1024)}, u32[]{:S(2)}) copy-start(f32[2304]{0:T(1024)} %param.22) | copy-start | bytes 27652
  50.8 75.5 %all-gather.4.cloned.1.call-start = ((), (), s32[]{:S(2)}) async-start(), calls=%async_computation.1 | async-start | bytes 10948608 | tf_op jit(solution)/shard_map/all_gather | solution.py:101
  51.4 123.6 %all-gather.6.cloned.1.call-start = ((), (), s32[]{:S(2)}) async-start(), calls=%async_computation.2 | async-start | bytes 10948608 | tf_op jit(solution)/shard_map/all_gather | solution.py:105
  51.9 182.7 %all-gather.8.cloned.1.call-start = ((), (), s32[]{:S(2)}) async-start(), calls=%async_computation.3 | async-start | bytes 10948608 | tf_op jit(solution)/shard_map/all_gather | solution.py:110
  52.5 257.1 %all-reduce.5.cloned.1.call-start = ((), (), s32[]{:S(2)}) async-start(), calls=%async_computation.4 | async-start | bytes 4866048 | tf_op jit(solution)/shard_map/psum | solution.py:116
  120.5 5.8 %copy-start.6 = (f32[2304]{0:T(1024)S(1)}, f32[2304]{0:T(1024)}, u32[]{:S(2)}) copy-start(f32[2304]{0:T(1024)} %param.23) | copy-start | bytes 27652
  311.8 5.4 %copy-start.1 = (bf16[512,2304]{1,0:T(8,128)(2,1)S(1)}, bf16[512,2304]{1,0:T(8,128)(2,1)}, u32[]{:S(2)}) copy-start(bf16[512,2304]{1,0:T(8,128)(2,1)} %param.21) | copy-start | bytes 7077892
Sparse Core Ops, SparseCore 0:
  50.9 67.3 all-reduce.2
  246.4 63.1 all-reduce.4
Sparse Core Ops, SparseCore 1:
  53.6 61.6 all-gather.3
  117.4 57.5 all-gather.5
  177.2 57.4 all-gather.7
where the time goes:
time: 325 us
  waiting for transfers between devices  213 us (66%)
  matrix products  63.9 us (20%)
  other arithmetic  20.2 us (6%)
  between operations  15.9 us (5%)
  local copies, waits for them, and re-layouts  12 us (4%)
    psum x1, waiting for transfers between devices, per_device(): lax.psum(jnp.dot(attended, o_weight, preferred_element_type=jnp.float32)....  65.7 us
    psum x1, waiting for transfers between devices, per_device(): lax.psum(partial_out.astype(jnp.bfloat16), 'mlp').astype(jnp.float32)  62.5 us
    all_gather x1, waiting for transfers between devices, per_device(): lax.all_gather(w_down, 'req', axis=0, tiled=True)  46.8 us
    all_gather x1, waiting for transfers between devices, per_device(): lax.all_gather(w_up, 'req', axis=0, tiled=True)  36 us
    dot_general x1, matrix products, per_device(): jnp.dot(normed, lax.all_gather(w_up, 'req', axis=0, tiled=True), preferre...  12.9 us
    dot_general x1, matrix products, per_device(): jnp.dot(normed, lax.all_gather(w_gate, 'req', axis=0, tiled=True), prefer...  12.7 us
    dot_general x1, matrix products, per_device(): lax.dot_general(act, lax.all_gather(w_down, 'req', axis=0, tiled=True), (...  11.6 us
    dot_general x1, matrix products, attend(): jnp.einsum('rghd,tgd->rght', pre_q, pre_keys, preferred_element_type=jnp....  10.4 us
  transfers between devices with their start and end apart: 5, of which 4 were waited for; matrix products, arithmetic and copies ran while one was open for 11% of the time, Pallas kernels for 0%

commit v1 on v0

--- a/solution.py
+++ b/solution.py
@@ -113,7 +113,12 @@
     )
     width = hidden_in.shape[1] // lax.axis_size("mlp")
     first = lax.axis_index("mlp") * width
-    total = lax.psum(partial_out.astype(jnp.bfloat16), "mlp").astype(jnp.float32)
+
+    def figure_proceed(u_in, net_axis):
+        frame_out = lax.all_gather(u_in, net_axis).sum(axis=0)
+        return frame_out
+
+    total = figure_proceed(partial_out.astype(jnp.bfloat16), "mlp").astype(jnp.float32)
     combined = resid + rms(total, ffn_out_gain)
     result = lax.dynamic_slice_in_dim(combined, first, width, 1)
     return result.astype(jnp.bfloat16)

time: 325 us -> 361 us (1.11)
  waiting for transfers between devices: 213 us -> 243 us
  other arithmetic: 20.2 us -> 26 us
    all_gather x0 -> x1, waiting for transfers between devices: none -> 92.7 us  [figure_proceed(): frame_out = lax.all_gather(u_in, net_axis).sum(axis=0)]
    psum x1 -> x0, waiting for transfers between devices: 62.5 us -> none  [per_device(): lax.psum(partial_out.astype(jnp.bfloat16), 'mlp').astype(jnp.float32)]
    reduce_sum x0 -> x1, other arithmetic: none -> 7.56 us  [figure_proceed(): frame_out = lax.all_gather(u_in, net_axis).sum(axis=0)]
  transfers between devices with their start and end apart: 5 -> 5, of which waited for: 4 -> 4; matrix products, arithmetic and copies ran while one was open for 11% -> 10% of each run, Pallas kernels for 0% -> 0%
where the time goes in v1:
time: 361 us
  waiting for transfers between devices  243 us (67%)
  matrix products  63.9 us (18%)
  other arithmetic  26 us (7%)
  between operations  15.9 us (4%)
  local copies, waits for them, and re-layouts  12.3 us (3%)
    all_gather x1, waiting for transfers between devices, figure_proceed(): frame_out = lax.all_gather(u_in, net_axis).sum(axis=0)  92.7 us
    psum x1, waiting for transfers between devices, per_device(): lax.psum(jnp.dot(attended, o_weight, preferred_element_type=jnp.float32)....  65.7 us
    all_gather x1, waiting for transfers between devices, per_device(): lax.all_gather(w_down, 'req', axis=0, tiled=True)  46.8 us
    all_gather x1, waiting for transfers between devices, per_device(): lax.all_gather(w_up, 'req', axis=0, tiled=True)  36 us
    dot_general x1, matrix products, per_device(): jnp.dot(normed, lax.all_gather(w_up, 'req', axis=0, tiled=True), preferre...  12.9 us
    dot_general x1, matrix products, per_device(): jnp.dot(normed, lax.all_gather(w_gate, 'req', axis=0, tiled=True), prefer...  12.7 us
    dot_general x1, matrix products, per_device(): lax.dot_general(act, lax.all_gather(w_down, 'req', axis=0, tiled=True), (...  11.6 us
    dot_general x1, matrix products, attend(): jnp.einsum('rghd,tgd->rght', pre_q, pre_keys, preferred_element_type=jnp....  10.4 us
  transfers between devices with their start and end apart: 5, of which 4 were waited for; matrix products, arithmetic and copies ran while one was open for 10% of the time, Pallas kernels for 0%

profile of v1, /device:TPU:1, one launch (start us, length us, event | category | flops | bytes accessed | tf_op | source)
XLA Modules:
  0.0 361.0 jit_solution(14327271495713828298)
XLA Ops:
  7.4 0.8 fusion.41
  8.2 0.7 slice.17
  8.9 1.1 slice.16
  10.7 3.0 iota_compare_fusion
  13.9 4.5 %gather_fusion.1 = bf16[32,128,256]{2,1,0:T(8,128)(2,1)} fusion(bf16[80,128,256]{2,1,0:T(8,128)(2,1)} %param.15, s32[1024]{0:T(1024)S(1)} %pad_clamp_fusion), kind=kCustom, calls=%fused_computation.1 | custom fusion | bytes 4194432 | tf_op jit(solution)/shard_map/gather | solution.py:36
  18.4 4.5 %gather_fusion = bf16[32,128,256]{2,1,0:T(8,128)(2,1)} fusion(bf16[80,128,256]{2,1,0:T(8,128)(2,1)} %param.16, s32[1024]{0:T(1024)S(1)} %pad_clamp_fusion), kind=kCustom, calls=%fused_computation | custom fusion | bytes 4194432 | tf_op jit(solution)/shard_map/gather | solution.py:37
  23.0 0.2 select_reduce_fusion
  23.2 0.2 add.104
  23.5 0.3 fusion.35
  23.8 10.4 %fusion = (f32[512,2]{0,1:T(2,128)S(1)}, f32[4096,512,2]{1,0,2:T(8,128)}) fusion(pred[512,4096]{0,1:T(8,128)(4,1)} %iota_compare_fusion, bf16[4096,256,1]{1,0,2:T(8,128)(2,1)} %bitcast.103, bf16[512,2,256]{0,2,1:T(8,128)(2,1)S(1)} %bitcast.112), kind=kOutput, calls=%fused_computation.3 | convolution fusion | flops 2164259840 | bytes 21499904 | tf_op jit(solution)/shard_map/rghd,tgd->rght/dot_general | solution.py:40
  34.3 9.5 %fusion.32 = bf16[512,1,2,256]{0,3,2,1:T(8,128)(2,1)S(1)} fusion(bf16[4096,256,1]{1,0,2:T(8,128)(2,1)S(1)} %bitcast.102, f32[4096,512,2]{1,0,2:T(8,128)} %get-tuple-element.10, pred[512,4096]{0,1:T(8,128)(4,1)S(1)} %copy-done.3, f32[512,2]{0,1:T(2,128)S(1)} %get-tuple-element.9), kind=kOutput, calls=%fused_computation.45 | convolution fusion | flops 2164785152 | bytes 21499904 | tf_op jit(solution)/shard_map/rght,tgd->rghd/dot_general | solution.py:44
  43.9 1.8 fusion.47
  45.6 2.1 fusion.29
  47.9 2.9 convolution_convert_fusion.1
  50.8 0.5 all-gather.6.cloned.1.call-update
  51.4 0.5 all-gather.8.cloned.1.call-update
  52.0 0.5 all-gather.10.cloned.1.call-update
  52.6 65.7 %all-reduce.2.cloned.1.call-done = bf16[528,2304]{1,0:T(8,128)(2,1)} async-done(((bf16[528,2304]{1,0:T(8,128)(2,1)}), bf16[528,2304]{1,0:T(8,128)(2,1)}) %all-reduce.2.cloned.1.call-update) | async-done | bytes 2433040 | tf_op jit(solution)/shard_map/psum | solution.py:94
  118.2 2.2 fusion.11
  120.5 5.8 %multiply_reduce_fusion.1 = (f32[528]{0:T(1024)S(1)}, f32[528,2304]{1,0:T(8,128)}) fusion(f32[2304]{0:T(1024)S(1)} %copy-done.5, f32[528]{0:T(1024)S(1)} %add_rsqrt_fusion.2, bf16[528,2304]{1,0:T(8,128)(2,1)} %all-reduce.2.cloned.1.call-done, bf16[528,2304]{1,0:T(8,128)(2,1)} %param.20), kind=kLoop, calls=%fused_computation.31 | loop fusion | flops 8515056 | bytes 9745536 | tf_op jit(solution)/shard_map/reduce_sum | solution.py:17
  126.3 12.7 %fusion.45 = f32[528,2304]{1,0:T(8,128)} fusion(bf16[2304,2304]{1,0:T(8,128)(2,1)} %all-gather.6.cloned.1.call-done, f32[528,2304]{1,0:T(8,128)} %get-tuple-element.6, f32[2304]{0:T(1024)S(1)} %copy-done.7, f32[528]{0:T(1024)S(1)} %add_rsqrt_fusion.1), kind=kOutput, calls=%fused_computation.69 | convolution fusion | flops 5609336832 | bytes 20360256 | tf_op jit(solution)/shard_map/dot_general | solution.py:99
  139.0 36.0 %all-gather.8.cloned.1.call-done = bf16[2304,2304]{1,0:T(8,128)(2,1)} async-done(((bf16[72,2304]{1,0:T(8,128)(2,1)}), bf16[2304,2304]{1,0:T(8,128)(2,1)}) %all-gather.8.cloned.1.call-update) | async-done | bytes 10616848 | tf_op jit(solution)/shard_map/all_gather | solution.py:105
  174.9 12.9 %fusion.21 = bf16[528,2304]{1,0:T(8,128)(2,1)} fusion(bf16[2304,2304]{1,0:T(8,128)(2,1)} %all-gather.8.cloned.1.call-done, f32[528,2304]{1,0:T(8,128)} %fusion.45, f32[528,2304]{1,0:T(8,128)} %get-tuple-element.6, f32[2304]{0:T(1024)S(1)} %copy-done.7, f32[528]{0:T(1024)S(1)} %add_rsqrt_fusion.1), kind=kOutput, calls=%fused_computation.32 | convolution fusion | flops 5621501952 | bytes 22793280 | tf_op jit(solution)/shard_map/dot_general | solution.py:104
  187.8 46.8 %all-gather.10.cloned.1.call-done = bf16[2304,2304]{1,0:T(8,128)(2,1)} async-done(((bf16[72,2304]{1,0:T(8,128)(2,1)}), bf16[2304,2304]{1,0:T(8,128)(2,1)}) %all-gather.10.cloned.1.call-update) | async-done | bytes 10616848 | tf_op jit(solution)/shard_map/all_gather | solution.py:110
  234.6 11.6 %convolution_convert_fusion = bf16[528,2304]{1,0:T(8,128)(2,1)} fusion(bf16[528,2304]{1,0:T(8,128)(2,1)} %fusion.21, bf16[2304,2304]{1,0:T(8,128)(2,1)} %all-gather.10.cloned.1.call-done), kind=kOutput, calls=%fused_computation.33 | convolution fusion | flops 5606903808 | bytes 15482880 | tf_op jit(solution)/shard_map/dot_general | solution.py:108
  246.2 0.8 dynamic-slice
  247.0 92.7 %all-gather.12.cloned.1.call-done = bf16[2112,2304]{1,0:T(8,128)(2,1)} async-done(((bf16[528,2304]{1,0:T(8,128)(2,1)}), bf16[2112,2304]{1,0:T(8,128)(2,1)}) %all-gather.12.cloned.1.call-update) | async-done | bytes 9732112 | tf_op jit(solution)/shard_map/all_gather | solution.py:118
  339.7 7.6 %reduce_sum.61 = bf16[528,2304]{1,0:T(8,128)(2,1)} reduce(bf16[4,528,2304]{2,1,0:T(8,128)(2,1)} %bitcast.100, bf16[]{:T(256)} %constant.18.clone.1), dimensions={0}, to_apply=%region_6.7 | reduce | flops 3649536 | bytes 12165122 | tf_op jit(solution)/shard_map/reduce_sum | solution.py:118
  347.3 2.2 convert_element_type.56
  349.5 0.2 copy-done.2
  349.7 0.5 multiply_reduce_fusion
  350.2 3.2 fusion.25
  (45 shorter events, 0.7 us)
Async XLA Ops:
  7.4 40.5 %copy-start = (bf16[512,2304]{1,0:T(8,128)(2,1)S(1)}, bf16[512,2304]{1,0:T(8,128)(2,1)}, u32[]{:S(2)}) copy-start(bf16[512,2304]{1,0:T(8,128)(2,1)} %param.21) | copy-start | bytes 7077892
  7.4 110.8 %all-reduce.2.cloned.1.call-start = ((), (), s32[]{:S(2)}) async-start(), calls=%async_computation | async-start | bytes 4866048 | tf_op jit(solution)/shard_map/psum | solution.py:94
  13.7 9.2 %copy-start.6 = (s32[16]{0:T(128)S(1)}, s32[16]{0:T(128)}, u32[]{:S(2)}) copy-start(s32[16]{0:T(128)} %param.17) | copy-start | bytes 196
  23.7 10.5 %copy-start.3 = (pred[512,4096]{0,1:T(8,128)(4,1)S(1)}, pred[512,4096]{0,1:T(8,128)(4,1)}, u32[]{:S(2)}) copy-start(pred[512,4096]{0,1:T(8,128)(4,1)} %iota_compare_fusion) | copy-start | bytes 6291460
  23.7 10.5 %copy-start.4 = (bf16[32,128,256]{2,1,0:T(8,128)(2,1)S(1)}, bf16[32,128,256]{2,1,0:T(8,128)(2,1)}, u32[]{:S(2)}) copy-start(bf16[32,128,256]{2,1,0:T(8,128)(2,1)} %gather_fusion) | copy-start | bytes 6291460
  23.7 20.1 %slice-start = ((s8[5242880]{0:T(1024)(128)(4,1)}), s8[4194304]{0:T(1024)(128)(4,1)S(1)}, s32[]{:S(2)}) async-start(s8[5242880]{0:T(1024)(128)(4,1)} %bitcast.104), calls=%async_computation.5 | async-start | bytes 8388608
  23.8 21.9 %slice-start.2 = ((s8[5242880]{0:T(1024)(128)(4,1)}), s8[4194304]{0:T(1024)(128)(4,1)S(1)}, s32[]{:S(2)}) async-start(s8[5242880]{0:T(1024)(128)(4,1)} %bitcast.107), calls=%async_computation.7 | async-start | bytes 8388608
  34.2 9.6 %slice-start.1 = ((s8[5242880]{0:T(1024)(128)(4,1)}), s8[1048576]{0:T(1024)(128)(4,1)S(1)}, s32[]{:S(2)}) async-start(s8[5242880]{0:T(1024)(128)(4,1)} %bitcast.104), calls=%async_computation.6 | async-start | bytes 2097152
  34.2 9.6 %slice-start.4 = ((bf16[528,512]{1,0:T(8,128)(2,1)}), bf16[16,512]{1,0:T(8,128)(2,1)S(1)}, s32[]{:S(2)}) async-start(bf16[528,512]{1,0:T(8,128)(2,1)} %param.14), calls=%async_computation.9 | async-start | bytes 32768 | tf_op jit(solution)/shard_map/slice | solution.py:34
  34.2 11.4 %slice-start.3 = ((s8[5242880]{0:T(1024)(128)(4,1)}), s8[1048576]{0:T(1024)(128)(4,1)S(1)}, s32[]{:S(2)}) async-start(s8[5242880]{0:T(1024)(128)(4,1)} %bitcast.107), calls=%async_computation.8 | async-start | bytes 2097152
  50.7 69.7 %copy-start.5 = (f32[2304]{0:T(1024)S(1)}, f32[2304]{0:T(1024)}, u32[]{:S(2)}) copy-start(f32[2304]{0:T(1024)} %param.22) | copy-start | bytes 27652
  50.8 75.5 %all-gather.6.cloned.1.call-start = ((), (), s32[]{:S(2)}) async-start(), calls=%async_computation.1 | async-start | bytes 10948608 | tf_op jit(solution)/shard_map/all_gather | solution.py:101
  51.3 123.6 %all-gather.8.cloned.1.call-start = ((), (), s32[]{:S(2)}) async-start(), calls=%async_computation.2 | async-start | bytes 10948608 | tf_op jit(solution)/shard_map/all_gather | solution.py:105
  51.9 182.7 %all-gather.10.cloned.1.call-start = ((), (), s32[]{:S(2)}) async-start(), calls=%async_computation.3 | async-start | bytes 10948608 | tf_op jit(solution)/shard_map/all_gather | solution.py:110
  52.5 287.2 %all-gather.12.cloned.1.call-start = ((), (), s32[]{:S(2)}) async-start(), calls=%async_computation.4 | async-start | bytes 12165120 | tf_op jit(solution)/shard_map/all_gather | solution.py:118
  120.5 5.8 %copy-start.7 = (f32[2304]{0:T(1024)S(1)}, f32[2304]{0:T(1024)}, u32[]{:S(2)}) copy-start(f32[2304]{0:T(1024)} %param.23) | copy-start | bytes 27652
  339.7 13.7 %copy-start.1 = (bf16[512,2304]{1,0:T(8,128)(2,1)S(1)}, bf16[512,2304]{1,0:T(8,128)(2,1)}, u32[]{:S(2)}) copy-start(bf16[512,2304]{1,0:T(8,128)(2,1)} %param.21) | copy-start | bytes 7077892
  347.3 2.4 copy-start.2
Sparse Core Ops, SparseCore 0:
  50.9 67.2 all-reduce.1
  246.4 93.2 all-gather.11
Sparse Core Ops, SparseCore 1:
  53.6 61.6 all-gather.5
  117.4 57.4 all-gather.7
  177.1 57.4 all-gather.9
